TPU v7x, 32 devices: a whole 2x2x4 slice. The times are simulated.
32 devices in a mesh: row: 8 (over y, x, core), col: 4 (over z).
Axes of the slice: x: 2, y: 2, z: 4, core: 2. Of those that a mesh axis runs over, the one named last changes fastest.
Arguments:
- features: bfloat16 [512, 16384], P('col', 'row'), may hold values from -6 to 6
- weight: bfloat16 [512, 512], replicated, may hold values from -0.25 to 0.25
- tile_cols: int32 [8, 256], P('row'), may hold values from 0 to 127, as said below
- tile_rows: int32 [8, 256], P('row'), may hold values from 0 to 15
- tile_count: int32 [8], P('row'), may hold values from 1 to 256, as said below
- tile_values: bfloat16 [2048, 128, 128], P('row'), may hold values from 0 to 0.049804688
- out_grad: bfloat16 [512, 16384], P('col', 'row'), may hold values from -6 to 6
Outputs:
- output: bfloat16 [512, 16384], P('col', 'row')
- input_grad: bfloat16 [512, 16384], P('col', 'row')
- weight_grad: float32 [512, 512], P(None, 'col')
Inputs may be any that keep to these rules, and one draw needn't show every extreme that they name: `tile_cols`: the column tiles used by the slots t < tile_count[r] of row index r that lie in the range of one other row index s (tiles s * 16 to s * 16 + 15) are at most 4 distinct ones, and some pair r, s has exactly 4. Slots past tile_count[r] hold in-range entries that are not used. `tile_count`: some row index uses all 256 slots.
All inputs are finite; a program needn't handle non-finite values.
Results may differ from a plain program's by a relative error of at most 0.0061.
Values may be sent and summed in bfloat16 or wider, within the bound.
No kernel may reach another device: no remote copies, remote signals or barrier semaphores. Data moves between devices by JAX's collectives and lax.ppermute only.
A program may use at most 128 MiB of HBM per device.

v0:
```python
import jax
import jax.numpy as jnp
from jax import lax
from jax.sharding import PartitionSpec as P

TILE = 128


def shards(features, weight, tile_cols, tile_rows, tile_count, tile_values, out_grad):
    n_row = lax.axis_size("row")
    col_self = lax.axis_index("col")
    f_loc, nodes_loc = features.shape
    h_loc = out_grad.shape[0]
    row_tiles = nodes_loc // TILE
    max_tiles = tile_cols.shape[1]
    col_ids = tile_cols[0]
    row_ids = tile_rows[0]
    slot_ids = jnp.arange(max_tiles, dtype=jnp.int32)
    in_use = slot_ids < tile_count[0]
    all_feats = lax.all_gather(features, "col", axis=0, tiled=True)
    w_mine = lax.dynamic_slice_in_dim(weight, col_self * h_loc, h_loc, 1)
    projected = jnp.einsum("fh,fn->hn", w_mine, all_feats, preferred_element_type=jnp.float32)
    projected = projected.astype(jnp.bfloat16).reshape(h_loc, row_tiles, TILE)
    sources_table = lax.all_gather(projected, "row", axis=1, tiled=True)
    picked = jnp.take(sources_table, col_ids, axis=1)
    products = jnp.einsum("htm,tnm->thn", picked, tile_values, preferred_element_type=jnp.float32)
    placing = (
        (row_ids[:, None] == jnp.arange(row_tiles, dtype=jnp.int32)[None, :]) & in_use[:, None]
    ).astype(jnp.float32)
    preact = jnp.einsum("ti,thn->hin", placing, products, precision=lax.Precision.HIGHEST)
    logistic = jax.nn.sigmoid(preact)
    output = (preact * logistic).astype(jnp.bfloat16)
    slope_v = logistic * (1.0 + preact * (1.0 - logistic))
    z_grad = (out_grad.reshape(h_loc, row_tiles, TILE).astype(jnp.float32) * slope_v).astype(
        jnp.bfloat16
    )
    picked_z = jnp.take(z_grad, row_ids, axis=1)
    back_terms = jnp.einsum(
        "htn,tnm->thm", picked_z, tile_values, preferred_element_type=jnp.float32
    )
    back_terms = back_terms * in_use.astype(jnp.float32)[:, None, None]
    spread = jax.ops.segment_sum(back_terms, col_ids, num_segments=n_row * row_tiles)
    summed = lax.psum_scatter(spread, "row", scatter_dimension=0, tiled=True)
    p_grad = summed.astype(jnp.bfloat16)
    w_term = jnp.einsum(
        "fbn,bhn->fh",
        all_feats.reshape(all_feats.shape[0], row_tiles, TILE),
        p_grad,
        preferred_element_type=jnp.float32,
    )
    weight_grad = lax.psum(w_term, "row") * float(nodes_loc * n_row) ** (-0.5)
    w_rows = lax.dynamic_slice_in_dim(weight, col_self * f_loc, f_loc, 0)
    grad_sum = jnp.einsum(
        "fh,bhn->fbn",
        w_rows,
        lax.all_gather(p_grad, "col", axis=1, tiled=True),
        preferred_element_type=jnp.float32,
    )
    input_grad = grad_sum.astype(jnp.bfloat16).reshape(f_loc, nodes_loc)
    return (output.reshape(h_loc, nodes_loc), input_grad, weight_grad)


def solution(mesh):
    return jax.shard_map(
        shards,
        mesh=mesh,
        in_specs=(
            P("col", "row"),
            P(),
            P("row", None),
            P("row", None),
            P("row"),
            P("row", None, None),
            P("col", "row"),
        ),
        out_specs=(P("col", "row"), P("col", "row"), P(None, "col")),
        check_vma=False,
    )
```

profile of v0, /device:TPU:0, one launch (start us, length us, event | category | flops | bytes accessed | tf_op | source)
XLA Modules:
  0.0 408.7 jit_solution(3409858486664761841)
XLA Ops:
  7.2 0.0 copy-start
  7.2 0.0 copy-start.3
  7.2 0.0 copy-start.4
  7.2 0.0 all-gather.4.cloned.1.call-start
  7.2 2.1 copy.22
  9.3 0.0 all-gather.4.cloned.1.call-update
  9.4 0.0 all-gather.6.cloned.1.call-start
  9.4 49.7 %all-gather.4.cloned.1.call-done = bf16[512,2048]{0,1:T(8,128)(2,1)} async-done(((bf16[128,2048]{0,1:T(8,128)(2,1)}), bf16[512,2048]{0,1:T(8,128)(2,1)}) %all-gather.4.cloned.1.call-update) | async-done | bytes 2097168 | tf_op jit(solution)/shard_map/all_gather | solution.py:20
  59.1 0.0 copy-done
  59.1 2.4 fusion.14
  61.6 0.9 copy.45
  62.5 0.0 all-gather.6.cloned.1.call-update
  62.5 0.0 reduce-scatter.2.cloned.1.call-start
  63.2 1.1 convert_bitcast_fusion
  64.4 0.2 copy.35
  64.6 0.0 copy-done.3
  64.6 0.0 copy-done.4
  64.7 33.0 %all-gather.6.cloned.1.call-done = bf16[128,128,128]{2,0,1:T(8,128)(2,1)} async-done(((bf16[128,16,128]{2,0,1:T(8,128)(2,1)}), bf16[128,128,128]{2,0,1:T(8,128)(2,1)}) %all-gather.6.cloned.1.call-update) | async-done | bytes 4194320 | tf_op jit(solution)/shard_map/all_gather | solution.py:24
  97.6 10.8 %gather_fusion = bf16[256,128,128]{2,1,0:T(8,128)(2,1)} fusion(bf16[128,128,128]{2,0,1:T(8,128)(2,1)} %all-gather.6.cloned.1.call-done, s32[1024]{0:T(1024)S(1)} %pad_clamp_fusion.1), kind=kCustom, calls=%fused_computation | custom fusion | bytes 16778240 | tf_op jit(solution)/shard_map/jit(_take)/gather | solution.py:25
  108.4 12.8 %fusion.3 = f32[256,128,128]{2,1,0:T(8,128)} fusion(bf16[256,128,128]{2,1,0:T(8,128)(2,1)} %param.12, bf16[256,128,128]{2,1,0:T(8,128)(2,1)} %gather_fusion, pred[256]{0:T(512)(128)(4,1)S(1)} %compare_and_fusion.1), kind=kOutput, calls=%fused_computation.7 | convolution fusion | flops 1077936128 | bytes 33554688 | tf_op jit(solution)/shard_map/htm,tnm->thn/dot_general | solution.py:26
  121.2 14.1 %fusion.15 = (bf16[128,16,128]{2,1,0:T(8,128)(2,1)S(1)}, bf16[128,16,128]{2,1,0:T(8,128)(2,1)}) fusion(f32[16,8,16,128]{3,2,1,0:T(8,128)S(1)} %copy.35, s32[256]{0:T(256)S(1)} %bitcast.63, pred[256]{0:T(512)(128)(4,1)S(1)} %iota_compare_fusion.1, f32[256,128,128]{2,1,0:T(8,128)} %fusion.3), kind=kOutput, calls=%fused_computation.20 | convolution fusion | flops 808198144 | bytes 18875648 | tf_op jit(solution)/shard_map/ti,thn->hin/dot_general | solution.py:30
  135.3 0.1 copy.25
  135.4 8.6 %gather_fusion.1 = bf16[256,128,128]{2,1,0:T(8,128)(2,1)} fusion(bf16[128,16,128]{2,0,1:T(8,128)(2,1)S(1)} %copy.25, s32[1024]{0:T(1024)S(1)} %pad_clamp_fusion), kind=kCustom, calls=%fused_computation.1 | custom fusion | bytes 16778240 | tf_op jit(solution)/shard_map/jit(_take)/gather | solution.py:37
  144.1 14.0 %convolution_multiply_fusion = f32[256,128,128]{2,1,0:T(8,128)} fusion(bf16[256,128,128]{2,1,0:T(8,128)(2,1)} %param.12, bf16[256,128,128]{2,1,0:T(8,128)(2,1)} %gather_fusion.1, f32[256]{0:T(256)S(1)} %get-tuple-element.15, pred[256]{0:T(512)(128)(4,1)S(1)} %get-tuple-element.14), kind=kOutput, calls=%fused_computation.5 | convolution fusion | flops 1082130432 | bytes 33555712 | tf_op jit(solution)/shard_map/htn,tnm->thm/dot_general | solution.py:38
  158.1 4.3 %broadcast_in_dim.26 = f32[128,128,128]{2,1,0:T(8,128)} broadcast(f32[]{:T(128)} %constant.40.clone.1), dimensions={} | broadcast | bytes 8388612 | tf_op jit(solution)/shard_map/broadcast_in_dim | solution.py:42
  162.4 51.3 %scatter_fusion = f32[128,128,128]{2,1,0:T(8,128)} fusion(f32[128,128,128]{2,1,0:T(8,128)} %broadcast_in_dim.26, s32[256]{0:T(256)S(1)} %bitcast.65, f32[256,128,128]{2,1,0:T(8,128)} %convolution_multiply_fusion), kind=kCustom, calls=%fused_computation.2 | custom fusion | flops 4194304 | bytes 50332672 | tf_op jit(solution)/shard_map/scatter-add | solution.py:42
  213.6 9.0 %copy.26 = f32[128,128,128]{1,2,0:T(8,128)} copy(f32[128,128,128]{2,1,0:T(8,128)} %scatter_fusion) | data formatting | bytes 16777216 | tf_op jit(solution)/shard_map/scatter-add | solution.py:42
  222.6 0.0 copy-start.1
  222.6 0.0 reduce-scatter.2.cloned.1.call-update
  222.7 0.0 all-reduce.2.cloned.1.call-start
  222.7 71.6 %reduce-scatter.2.cloned.1.call-done = f32[16,128,128]{1,2,0:T(8,128)} async-done(((f32[128,128,128]{1,2,0:T(8,128)}), f32[16,128,128]{1,2,0:T(8,128)}) %reduce-scatter.2.cloned.1.call-update) | async-done | bytes 1048592 | tf_op jit(solution)/shard_map/reduce_scatter | solution.py:43
  294.3 1.3 convert_element_type.35
  295.6 0.0 copy-start.2
  295.6 0.0 copy-done.1
  295.6 1.2 convolution_bitcast_fusion
  296.8 0.0 all-reduce.2.cloned.1.call-update
  296.8 0.0 all-gather.8.cloned.1.call-start
  296.9 0.0 copy-done.2
  296.9 0.5 all-gather.8.cloned.1.call-update
  297.4 2.0 copy.44
  299.4 52.3 %all-reduce.2.cloned.1.call-done = f32[512,128]{0,1:T(8,128)} async-done(((f32[512,128]{0,1:T(8,128)}), f32[512,128]{0,1:T(8,128)}) %all-reduce.2.cloned.1.call-update) | async-done | bytes 262160 | tf_op jit(solution)/shard_map/psum | solution.py:51
  351.7 1.0 broadcast_multiply_fusion
  352.6 0.8 copy.30
  353.5 45.3 %all-gather.8.cloned.1.call-done = bf16[16,512,128]{1,2,0:T(8,128)(2,1)} async-done(((bf16[16,128,128]{1,2,0:T(8,128)(2,1)}), bf16[16,512,128]{1,2,0:T(8,128)(2,1)}) %all-gather.8.cloned.1.call-update) | async-done | bytes 2097168 | tf_op jit(solution)/shard_map/all_gather | solution.py:56
  398.7 2.3 fusion.16
  401.0 0.1 convert_element_type.36
  401.1 1.0 copy.29
  (7 shorter events, 0.0 us)
Async XLA Ops:
  7.2 52.0 %copy-start = (bf16[512,512]{1,0:T(8,128)(2,1)S(1)}, bf16[512,512]{1,0:T(8,128)(2,1)}, u32[]{:S(2)}) copy-start(bf16[512,512]{1,0:T(8,128)(2,1)} %param.8) | copy-start | bytes 1572868
  7.2 57.4 %copy-start.3 = (s32[1,256]{1,0:T(1,128)S(1)}, s32[1,256]{1,0:T(1,128)}, u32[]{:S(2)}) copy-start(s32[1,256]{1,0:T(1,128)} %param.10) | copy-start | bytes 3076
  7.2 57.4 %copy-start.4 = (s32[1,256]{1,0:T(1,128)S(1)}, s32[1,256]{1,0:T(1,128)}, u32[]{:S(2)}) copy-start(s32[1,256]{1,0:T(1,128)} %param.9) | copy-start | bytes 3076
  7.2 51.9 %all-gather.4.cloned.1.call-start = ((), (), s32[]{:S(2)}) async-start(), calls=%async_computation.1 | async-start | bytes 2621440 | tf_op jit(solution)/shard_map/all_gather | solution.py:20
  9.4 88.3 %all-gather.6.cloned.1.call-start = ((), (), s32[]{:S(2)}) async-start(), calls=%async_computation.2 | async-start | bytes 4718592 | tf_op jit(solution)/shard_map/all_gather | solution.py:24
  62.5 231.8 %reduce-scatter.2.cloned.1.call-start = ((), (), s32[]{:S(2)}) async-start(), calls=%async_computation.3 | async-start | bytes 9437184 | tf_op jit(solution)/shard_map/reduce_scatter | solution.py:43
  222.6 73.0 %copy-start.1 = (bf16[512,2048]{0,1:T(8,128)(2,1)S(1)}, bf16[512,2048]{0,1:T(8,128)(2,1)}, u32[]{:S(2)}) copy-start(bf16[512,2048]{0,1:T(8,128)(2,1)} %all-gather.4.cloned.1.call-done) | copy-start | bytes 6291460
  222.7 129.0 %all-reduce.2.cloned.1.call-start = ((), (), s32[]{:S(2)}) async-start(), calls=%async_computation.5 | async-start | bytes 524288 | tf_op jit(solution)/shard_map/psum | solution.py:51
  295.6 1.3 copy-start.2
  296.8 101.9 %all-gather.8.cloned.1.call-start = ((), (), s32[]{:S(2)}) async-start(), calls=%async_computation.4 | async-start | bytes 2621440 | tf_op jit(solution)/shard_map/all_gather | solution.py:56
Sparse Core Ops, SparseCore 0:
  10.2 48.9 all-gather.3
  62.6 34.9 all-gather.5
  222.8 71.4 reduce-scatter.1
  298.1 53.5 all-reduce.1
  353.1 45.6 all-gather.7
where the time goes:
time: 410 us; the launch traced here: 409 us
  waiting for transfers between devices  252 us (61%)
  other arithmetic  54.8 us (13%)
  matrix products  46.8 us (11%)
  local copies, waits for them, and re-layouts  39.9 us (10%)
  between operations  14.6 us (4%)
    reduce_scatter x1, waiting for transfers between devices, shards(): summed = lax.psum_scatter(spread, 'row', scatter_dimension=0, tiled=True)  71.6 us
    psum x1, waiting for transfers between devices, shards(): weight_grad = lax.psum(w_term, 'row') * float(nodes_loc * n_row) ** (-0.5)  52.3 us
    scatter-add x1, other arithmetic, shards(): jax.ops.segment_sum(back_terms, col_ids, num_segments=n_row * row_tiles)  51.3 us
    all_gather x1, waiting for transfers between devices, shards(): all_feats = lax.all_gather(features, 'col', axis=0, tiled=True)  49.7 us
    all_gather x1, waiting for transfers between devices, shards(): lax.all_gather(p_grad, 'col', axis=1, tiled=True)  45.3 us
    all_gather x1, waiting for transfers between devices, shards(): sources_table = lax.all_gather(projected, 'row', axis=1, tiled=True)  33 us
    dot_general x1, matrix products, shards(): jnp.einsum('ti,thn->hin', placing, products, precision=lax.Precision.HIGH...  14.1 us
    dot_general x1, matrix products, shards(): jnp.einsum('htn,tnm->thm', picked_z, tile_values, preferred_element_type=...  14 us
  transfers between devices with their start and end apart: 5, of which 5 were waited for; matrix products, arithmetic and copies ran while one was open for 1% of the time, Pallas kernels for 0%

commit v1 on v0

--- a/solution.py
+++ b/solution.py
@@ -48,7 +48,8 @@
         p_grad,
         preferred_element_type=jnp.float32,
     )
-    weight_grad = lax.psum(w_term, "row") * float(nodes_loc * n_row) ** (-0.5)
+    spread_the_region = lambda which_axis, field: jnp.sum(lax.all_gather(field, which_axis), 0)
+    weight_grad = spread_the_region("row", w_term) * float(nodes_loc * n_row) ** (-0.5)
     w_rows = lax.dynamic_slice_in_dim(weight, col_self * f_loc, f_loc, 0)
     grad_sum = jnp.einsum(
         "fh,bhn->fbn",

time: 410 us -> 383 us (0.934)
  waiting for transfers between devices: 252 us -> 223 us
    psum x1 -> x0, waiting for transfers between devices: 52.3 us -> none  [shards(): weight_grad = lax.psum(w_term, 'row') * float(nodes_loc * n_row) ** (-0.5)]
    all_gather x0 -> x1, waiting for transfers between devices: none -> 25.2 us  [shards(): lax.all_gather(field, which_axis)]
    unnamed x15 -> x14, local copies, waits for them, and re-layouts: 6.12 us -> 8.3 us
  transfers between devices with their start and end apart: 5 -> 5, of which waited for: 5 -> 5; matrix products, arithmetic and copies ran while one was open for 1% -> 2% of each run, Pallas kernels for 0% -> 0%
where the time goes in v1:
time: 383 us; the launch traced here: 382 us
  waiting for transfers between devices  223 us (58%)
  other arithmetic  55.3 us (14%)
  matrix products  47 us (12%)
  local copies, waits for them, and re-layouts  42 us (11%)
  between operations  14.6 us (4%)
    reduce_scatter x1, waiting for transfers between devices, shards(): summed = lax.psum_scatter(spread, 'row', scatter_dimension=0, tiled=True)  71.7 us
    scatter-add x1, other arithmetic, shards(): jax.ops.segment_sum(back_terms, col_ids, num_segments=n_row * row_tiles)  51.4 us
    all_gather x1, waiting for transfers between devices, shards(): all_feats = lax.all_gather(features, 'col', axis=0, tiled=True)  49.7 us
    all_gather x1, waiting for transfers between devices, shards(): lax.all_gather(p_grad, 'col', axis=1, tiled=True)  43.1 us
    all_gather x1, waiting for transfers between devices, shards(): sources_table = lax.all_gather(projected, 'row', axis=1, tiled=True)  33 us
    all_gather x1, waiting for transfers between devices, shards(): lax.all_gather(field, which_axis)  25.2 us
    dot_general x1, matrix products, shards(): jnp.einsum('htn,tnm->thm', picked_z, tile_values, preferred_element_type=...  14 us
    dot_general x1, matrix products, shards(): jnp.einsum('ti,thn->hin', placing, products, precision=lax.Precision.HIGH...  13.3 us
  transfers between devices with their start and end apart: 5, of which 5 were waited for; matrix products, arithmetic and copies ran while one was open for 2% of the time, Pallas kernels for 0%

profile of v1, /device:TPU:0, one launch (start us, length us, event | category | flops | bytes accessed | tf_op | source)
XLA Modules:
  0.0 382.1 jit_solution(467316190072736975)
XLA Ops:
  7.2 0.0 copy-start
  7.2 0.0 copy-start.2
  7.2 0.0 copy-start.3
  7.2 0.0 all-gather.6.cloned.1.call-start
  7.2 2.1 copy.20
  9.3 0.0 all-gather.6.cloned.1.call-update
  9.4 0.0 all-gather.8.cloned.1.call-start
  9.4 49.7 %all-gather.6.cloned.1.call-done = bf16[512,2048]{0,1:T(8,128)(2,1)} async-done(((bf16[128,2048]{0,1:T(8,128)(2,1)}), bf16[512,2048]{0,1:T(8,128)(2,1)}) %all-gather.6.cloned.1.call-update) | async-done | bytes 2097168 | tf_op jit(solution)/shard_map/all_gather | solution.py:20
  59.1 0.0 copy-done
  59.1 2.4 fusion.14
  61.6 0.9 copy.44
  62.5 0.0 all-gather.8.cloned.1.call-update
  62.5 0.0 reduce-scatter.2.cloned.1.call-start
  63.2 1.1 convert_bitcast_fusion
  64.4 0.2 copy.33
  64.6 0.0 copy-done.2
  64.6 0.0 copy-done.3
  64.7 33.0 %all-gather.8.cloned.1.call-done = bf16[128,128,128]{2,0,1:T(8,128)(2,1)} async-done(((bf16[128,16,128]{2,0,1:T(8,128)(2,1)}), bf16[128,128,128]{2,0,1:T(8,128)(2,1)}) %all-gather.8.cloned.1.call-update) | async-done | bytes 4194320 | tf_op jit(solution)/shard_map/all_gather | solution.py:24
  97.6 10.8 %gather_fusion = bf16[256,128,128]{2,1,0:T(8,128)(2,1)} fusion(bf16[128,128,128]{2,0,1:T(8,128)(2,1)} %all-gather.8.cloned.1.call-done, s32[1024]{0:T(1024)S(1)} %pad_clamp_fusion.1), kind=kCustom, calls=%fused_computation | custom fusion | bytes 16778240 | tf_op jit(solution)/shard_map/jit(_take)/gather | solution.py:25
  108.4 12.8 %fusion.3 = f32[256,128,128]{2,1,0:T(8,128)} fusion(bf16[256,128,128]{2,1,0:T(8,128)(2,1)} %param.12, bf16[256,128,128]{2,1,0:T(8,128)(2,1)} %gather_fusion, pred[256]{0:T(512)(128)(4,1)S(1)} %compare_and_fusion.1), kind=kOutput, calls=%fused_computation.7 | convolution fusion | flops 1077936128 | bytes 33554688 | tf_op jit(solution)/shard_map/htm,tnm->thn/dot_general | solution.py:26
  121.2 13.3 %fusion.15 = (bf16[128,16,128]{2,1,0:T(8,128)(2,1)S(1)}, bf16[128,16,128]{2,1,0:T(8,128)(2,1)S(1)}) fusion(f32[16,8,16,128]{3,2,1,0:T(8,128)S(1)} %copy.33, s32[256]{0:T(256)S(1)} %bitcast.69, pred[256]{0:T(512)(128)(4,1)S(1)} %iota_compare_fusion.1, f32[256,128,128]{2,1,0:T(8,128)} %fusion.3), kind=kOutput, calls=%fused_computation.21 | convolution fusion | flops 808198144 | bytes 18875648 | tf_op jit(solution)/shard_map/ti,thn->hin/dot_general | solution.py:30
  134.5 0.1 copy.23
  134.6 8.6 %gather_fusion.1 = bf16[256,128,128]{2,1,0:T(8,128)(2,1)} fusion(bf16[128,16,128]{2,0,1:T(8,128)(2,1)S(1)} %copy.23, s32[1024]{0:T(1024)S(1)} %pad_clamp_fusion), kind=kCustom, calls=%fused_computation.1 | custom fusion | bytes 16778240 | tf_op jit(solution)/shard_map/jit(_take)/gather | solution.py:37
  143.2 14.0 %convolution_multiply_fusion = f32[256,128,128]{2,1,0:T(8,128)} fusion(bf16[256,128,128]{2,1,0:T(8,128)(2,1)} %param.12, bf16[256,128,128]{2,1,0:T(8,128)(2,1)} %gather_fusion.1, f32[256]{0:T(256)S(1)} %get-tuple-element.15, pred[256]{0:T(512)(128)(4,1)S(1)} %get-tuple-element.14), kind=kOutput, calls=%fused_computation.5 | convolution fusion | flops 1082130432 | bytes 33555712 | tf_op jit(solution)/shard_map/htn,tnm->thm/dot_general | solution.py:38
  157.3 4.3 %broadcast_in_dim.26 = f32[128,128,128]{2,1,0:T(8,128)} broadcast(f32[]{:T(128)} %constant.26.clone.1), dimensions={} | broadcast | bytes 8388612 | tf_op jit(solution)/shard_map/broadcast_in_dim | solution.py:42
  161.5 51.4 %scatter_fusion = f32[128,128,128]{2,1,0:T(8,128)} fusion(f32[128,128,128]{2,1,0:T(8,128)} %broadcast_in_dim.26, s32[256]{0:T(256)S(1)} %bitcast.71, f32[256,128,128]{2,1,0:T(8,128)} %convolution_multiply_fusion), kind=kCustom, calls=%fused_computation.2 | custom fusion | flops 4194304 | bytes 50332672 | tf_op jit(solution)/shard_map/scatter-add | solution.py:42
  212.9 9.0 %copy.24 = f32[128,128,128]{1,2,0:T(8,128)} copy(f32[128,128,128]{2,1,0:T(8,128)} %scatter_fusion) | data formatting | bytes 16777216 | tf_op jit(solution)/shard_map/scatter-add | solution.py:42
  221.9 0.0 copy-start.1
  222.0 0.0 reduce-scatter.2.cloned.1.call-update
  222.0 0.0 all-gather.10.cloned.1.call-start
  222.0 71.7 %reduce-scatter.2.cloned.1.call-done = f32[16,128,128]{1,2,0:T(8,128)} async-done(((f32[128,128,128]{1,2,0:T(8,128)}), f32[16,128,128]{1,2,0:T(8,128)}) %reduce-scatter.2.cloned.1.call-update) | async-done | bytes 1048592 | tf_op jit(solution)/shard_map/reduce_scatter | solution.py:43
  293.8 2.1 convert_element_type.35
  295.9 0.0 all-gather.10.cloned.1.call-update
  295.9 0.0 all-gather.12.cloned.1.call-start
  296.0 0.0 copy-done.1
  296.0 2.2 convolution_bitcast_fusion
  298.2 0.0 all-gather.12.cloned.1.call-update
  298.2 0.9 copy.43
  299.1 43.1 %all-gather.10.cloned.1.call-done = bf16[16,512,128]{1,2,0:T(8,128)(2,1)} async-done(((bf16[16,128,128]{1,2,0:T(8,128)(2,1)}), bf16[16,512,128]{1,2,0:T(8,128)(2,1)}) %all-gather.10.cloned.1.call-update) | async-done | bytes 2097168 | tf_op jit(solution)/shard_map/all_gather | solution.py:57
  342.3 2.3 fusion.16
  344.6 0.1 convert_element_type.36
  344.7 1.0 copy.27
  345.7 25.2 %all-gather.12.cloned.1.call-done = f32[4096,128]{0,1:T(8,128)} async-done(((f32[512,128]{0,1:T(8,128)}), f32[4096,128]{0,1:T(8,128)}) %all-gather.12.cloned.1.call-update) | async-done | bytes 2097168 | tf_op jit(solution)/shard_map/all_gather | solution.py:51
  370.9 3.2 copy.34
  374.2 0.5 bitcast_reduce_fusion
  374.7 0.8 copy.28
  (8 shorter events, 0.1 us)
Async XLA Ops:
  7.2 52.0 %copy-start = (bf16[512,512]{1,0:T(8,128)(2,1)S(1)}, bf16[512,512]{1,0:T(8,128)(2,1)}, u32[]{:S(2)}) copy-start(bf16[512,512]{1,0:T(8,128)(2,1)} %param.8) | copy-start | bytes 1572868
  7.2 57.4 %copy-start.2 = (s32[1,256]{1,0:T(1,128)S(1)}, s32[1,256]{1,0:T(1,128)}, u32[]{:S(2)}) copy-start(s32[1,256]{1,0:T(1,128)} %param.10) | copy-start | bytes 3076
  7.2 57.4 %copy-start.3 = (s32[1,256]{1,0:T(1,128)S(1)}, s32[1,256]{1,0:T(1,128)}, u32[]{:S(2)}) copy-start(s32[1,256]{1,0:T(1,128)} %param.9) | copy-start | bytes 3076
  7.2 51.9 %all-gather.6.cloned.1.call-start = ((), (), s32[]{:S(2)}) async-start(), calls=%async_computation.1 | async-start | bytes 2621440 | tf_op jit(solution)/shard_map/all_gather | solution.py:20
  9.4 88.3 %all-gather.8.cloned.1.call-start = ((), (), s32[]{:S(2)}) async-start(), calls=%async_computation.2 | async-start | bytes 4718592 | tf_op jit(solution)/shard_map/all_gather | solution.py:24
  62.5 231.3 %reduce-scatter.2.cloned.1.call-start = ((), (), s32[]{:S(2)}) async-start(), calls=%async_computation.3 | async-start | bytes 9437184 | tf_op jit(solution)/shard_map/reduce_scatter | solution.py:43
  221.9 74.0 %copy-start.1 = (bf16[512,2048]{0,1:T(8,128)(2,1)S(1)}, bf16[512,2048]{0,1:T(8,128)(2,1)}, u32[]{:S(2)}) copy-start(bf16[512,2048]{0,1:T(8,128)(2,1)} %all-gather.6.cloned.1.call-done) | copy-start | bytes 6291460
  222.0 120.3 %all-gather.10.cloned.1.call-start = ((), (), s32[]{:S(2)}) async-start(), calls=%async_computation.4 | async-start | bytes 2621440 | tf_op jit(solution)/shard_map/all_gather | solution.py:57
  295.9 75.0 %all-gather.12.cloned.1.call-start = ((), (), s32[]{:S(2)}) async-start(), calls=%async_computation.5 | async-start | bytes 2359296 | tf_op jit(solution)/shard_map/all_gather | solution.py:51
Sparse Core Ops, SparseCore 0:
  10.2 48.9 all-gather.5
  62.6 34.9 all-gather.7
  222.1 71.6 reduce-scatter.1
  296.0 46.1 all-gather.9
  344.8 26.1 all-gather.11
